TPU v7x, 32 devices: a whole 2x2x4 slice. The times are simulated.
32 devices in a mesh: parts: 2 (over y), clip: 4 (over x, core), tensor: 4 (over z).
Axes of the slice: x: 2, y: 2, z: 4, core: 2. Of those that a mesh axis runs over, the one named last changes fastest.
Arguments:
- clips: bfloat16 [32, 128, 4096], P(('parts', 'clip'), None, 'tensor'), parts along dimension 0, may hold values from -6 to 6
- targets: bfloat16 [32, 128, 4096], P(('parts', 'clip'), None, 'tensor'), parts along dimension 0, may hold values from -6 to 6
- lengths: int32 [32], P(('parts', 'clip')), parts along dimension 0, may hold values from 32 to 128, as said below
- gate_weight: bfloat16 [4096, 7168], P(None, 'tensor'), may hold values from -0.09375 to 0.09375
- up_weight: bfloat16 [4096, 7168], P(None, 'tensor'), may hold values from -0.09375 to 0.09375
- down_weight: bfloat16 [7168, 4096], P('tensor'), may hold values from -0.0625 to 0.0625
- proj_in: bfloat16 [64, 7168], P(None, 'tensor'), may hold values from -0.0625 to 0.0625
- proj_out: bfloat16 [64, 4096], replicated, may hold values from -0.09375 to 0.09375
- inv_hessian: bfloat16 [4096, 4096], P('clip', 'tensor'), may hold values from -0.2 to 2.2, as said below
- test_sketches: bfloat16 [4096, 4096], P('clip', 'tensor'), may hold values from -6 to 6
Outputs:
- scores: float32 [32, 4096], P(('parts', 'clip'), 'tensor'), parts along dimension 0
There are 2 independent parts, one for each index of `parts`. A program takes and returns all parts, laid end to end along the dimension named above; an argument that names none is the same for every part. Nothing has to cross between parts.
Inputs may be any that keep to these rules, and one draw needn't show every extreme that they name: `lengths`: every clip has between 32 and 128 valid tokens; in each part one clip has exactly 128 and another exactly 32. `inv_hessian`: the same matrix in both parts.
All inputs are finite; a program needn't handle non-finite values.
Results may differ from a plain program's by a relative error of at most 0.0066.
Values may be sent and summed in bfloat16 or wider, within the bound.
A program may use at most 192 MiB of HBM per device.

v0:
```python
import jax
import jax.numpy as jnp
from jax import lax
from jax.sharding import PartitionSpec as P


def on_device(
    clips,
    targets,
    lengths,
    gate_weight,
    up_weight,
    down_weight,
    proj_in,
    proj_out,
    inv_hessian,
    test_sketches,
):
    clip_count, slot_count, width_part = clips.shape
    row_count = clip_count * slot_count
    proj_size = proj_in.shape[0]
    flat_tokens = clips.reshape(row_count, width_part)
    piece = lax.all_gather(flat_tokens, "tensor", axis=1, tiled=True)
    gate_act = jnp.dot(piece, gate_weight, preferred_element_type=jnp.float32)
    up_act = jnp.dot(piece, up_weight, preferred_element_type=jnp.float32)
    hidden = (jax.nn.silu(gate_act) * up_act).astype(jnp.bfloat16)
    left_part = jnp.dot(hidden, proj_in.T, preferred_element_type=jnp.float32)
    tensor_pos = lax.axis_index("tensor")
    lens_float = lengths.astype(jnp.float32)
    partial_out = jnp.dot(hidden, down_weight, preferred_element_type=jnp.float32)
    outputs = lax.psum_scatter(partial_out, "tensor", scatter_dimension=1, tiled=True)
    position = jnp.arange(slot_count, dtype=jnp.int32)
    masked = (position[None, :] < lengths[:, None]).astype(jnp.float32) / lens_float[:, None]
    golden = targets.reshape(row_count, width_part).astype(jnp.float32)
    differ = jnp.clip(outputs - golden, -1.0, 1.0)
    grad_out = (differ * masked.reshape(row_count)[:, None]).astype(jnp.bfloat16)
    proj_cols = lax.dynamic_slice_in_dim(proj_out, tensor_pos * width_part, width_part, 1)
    right_part = jnp.dot(grad_out, proj_cols.T, preferred_element_type=jnp.float32)
    joined = lax.psum(jnp.concatenate([left_part, right_part], axis=1), "tensor")
    left_full = joined[:, :proj_size].reshape(clip_count, slot_count, proj_size)
    right_full = joined[:, proj_size:].reshape(clip_count, slot_count, proj_size)
    sketch = jnp.einsum("cti,ctk->cik", left_full, right_full, precision=lax.Precision.HIGHEST)
    flat_sketch = sketch.reshape(clip_count, proj_size * proj_size).astype(jnp.bfloat16)
    precond = jnp.dot(
        flat_sketch,
        lax.all_gather(inv_hessian, "clip", axis=0, tiled=True),
        preferred_element_type=jnp.float32,
    ).astype(jnp.bfloat16)
    partial_scores = lax.dot_general(
        precond,
        lax.all_gather(test_sketches, "clip", axis=0, tiled=True),
        (((1,), (1,)), ((), ())),
        preferred_element_type=jnp.float32,
    )
    return lax.psum_scatter(partial_scores, "tensor", scatter_dimension=1, tiled=True)


def solution(mesh):
    in_specs = (
        P(("parts", "clip"), None, "tensor"),
        P(("parts", "clip"), None, "tensor"),
        P(("parts", "clip")),
        P(None, "tensor"),
        P(None, "tensor"),
        P("tensor", None),
        P(None, "tensor"),
        P(),
        P("clip", "tensor"),
        P("clip", "tensor"),
    )
    out_specs = P(("parts", "clip"), "tensor")
    return jax.shard_map(
        on_device, mesh=mesh, in_specs=in_specs, out_specs=out_specs, check_vma=False
    )
```

profile of v0, /device:TPU:0, one launch (start us, length us, event | category | flops | bytes accessed | tf_op | source)
XLA Modules:
  0.0 461.4 jit_solution(14233535387168297329)
XLA Ops:
  7.4 0.0 copy-start
  7.4 0.0 all-gather.4.cloned.1.call-start
  7.4 0.7 all-gather.4.cloned.1.call-update
  8.1 0.0 reduce-scatter.5.cloned.1.call-start
  8.1 85.1 %all-gather.4.cloned.1.call-done = bf16[512,4096]{1,0:T(8,128)(2,1)} async-done(((bf16[512,1024]{1,0:T(8,128)(2,1)}), bf16[512,4096]{1,0:T(8,128)(2,1)}) %all-gather.4.cloned.1.call-update) | async-done | bytes 4194320 | tf_op jit(solution)/shard_map/all_gather | solution.py:23
  93.3 0.0 copy-start.3
  93.3 0.0 slice-start
  93.3 0.0 slice-start.1
  93.3 14.7 %fusion.10 = f32[512,1792]{1,0:T(8,128)} fusion(bf16[512,4096]{1,0:T(8,128)(2,1)} %all-gather.4.cloned.1.call-done, bf16[4096,1792]{1,0:T(8,128)(2,1)} %param.13), kind=kOutput, calls=%fused_computation.20 | convolution fusion | flops 7516192768 | bytes 22544384 | tf_op jit(solution)/shard_map/dot_general | solution.py:24
  107.9 0.0 copy-done.3
  107.9 0.0 slice-start.2
  107.9 0.0 slice-start.3
  107.9 12.8 %multiply_convert_fusion = bf16[512,1792]{1,0:T(8,128)(2,1)S(1)} fusion(f32[512,1792]{1,0:T(8,128)} %fusion.10, bf16[512,4096]{1,0:T(8,128)(2,1)S(1)} %copy-done.3, bf16[4096,1792]{1,0:T(8,128)(2,1)} %param.14), kind=kOutput, calls=%fused_computation.1 | convolution fusion | flops 7521697792 | bytes 24379392 | tf_op jit(solution)/shard_map/dot_general | solution.py:25
  120.8 0.0 slice-done
  120.8 0.0 slice-done.1
  120.8 0.0 slice-done.2
  120.8 0.0 slice-done.3
  120.8 9.9 %fusion.12 = f32[512,4096]{1,0:T(8,128)} fusion(bf16[512,1792]{1,0:T(8,128)(2,1)S(1)} %multiply_convert_fusion, bf16[1792,4096]{1,0:T(8,128)(2,1)S(1)} %bitcast.34), kind=kOutput, calls=%fused_computation.22 | convolution fusion | flops 7516192768 | bytes 24903680 | tf_op jit(solution)/shard_map/dot_general | solution.py:30
  130.8 0.0 copy-start.2
  130.8 0.0 copy-start.1
  130.8 0.0 reduce-scatter.5.cloned.1.call-update
  130.8 0.0 all-reduce.2.cloned.1.call-start
  130.9 0.6 copy-done.2
  131.4 0.1 divide_bitcast_fusion
  131.5 1.6 fusion.11
  133.1 140.9 %reduce-scatter.5.cloned.1.call-done = f32[512,1024]{1,0:T(8,128)} async-done(((f32[512,4096]{1,0:T(8,128)}), f32[512,1024]{1,0:T(8,128)}) %reduce-scatter.5.cloned.1.call-update) | async-done | bytes 2097168 | tf_op jit(solution)/shard_map/reduce_scatter | solution.py:31
  274.0 0.0 copy-done.1
  274.0 1.9 fusion.2
  275.9 0.0 copy-done
  275.9 0.4 fusion.7
  276.4 0.7 pad_maximum_fusion
  277.1 0.0 all-reduce.2.cloned.1.call-update
  277.1 0.0 all-gather.6.cloned.1.call-start
  277.2 0.5 all-gather.6.cloned.1.call-update
  277.7 0.0 all-gather.8.cloned.1.call-start
  277.7 0.5 all-gather.8.cloned.1.call-update
  278.3 0.2 reduce-scatter.7.cloned.1.call-start
  278.5 34.8 %all-reduce.2.cloned.1.call-done = f32[512,128]{0,1:T(8,128)} async-done(((f32[512,128]{0,1:T(8,128)}), f32[512,128]{0,1:T(8,128)}) %all-reduce.2.cloned.1.call-update) | async-done | bytes 262160 | tf_op jit(solution)/shard_map/psum | solution.py:39
  313.3 1.0 slice_bitcast_fusion.1
  314.3 0.3 convolution_convert_fusion
  314.6 0.1 convert_element_type.39
  314.7 23.4 %all-gather.6.cloned.1.call-done = bf16[4096,1024]{1,0:T(8,128)(2,1)} async-done(((bf16[1024,1024]{1,0:T(8,128)(2,1)}), bf16[4096,1024]{1,0:T(8,128)(2,1)}) %all-gather.6.cloned.1.call-update) | async-done | bytes 8388624 | tf_op jit(solution)/shard_map/all_gather | solution.py:46
  338.1 59.7 %all-gather.8.cloned.1.call-done = bf16[4096,1024]{1,0:T(8,128)(2,1)} async-done(((bf16[1024,1024]{1,0:T(8,128)(2,1)}), bf16[4096,1024]{1,0:T(8,128)(2,1)}) %all-gather.8.cloned.1.call-update) | async-done | bytes 8388624 | tf_op jit(solution)/shard_map/all_gather | solution.py:51
  397.8 10.6 %convolution_bitcast_fusion = f32[4096,4]{1,0:T(8,128)} fusion(bf16[4096,1024]{1,0:T(8,128)(2,1)} %all-gather.8.cloned.1.call-done, bf16[4,4096]{1,0:T(4,128)(2,1)S(1)} %convert_element_type.39, bf16[4096,1024]{1,0:T(8,128)(2,1)} %all-gather.6.cloned.1.call-done), kind=kOutput, calls=%fused_computation | convolution fusion | flops 67112960 | bytes 16875520
  408.4 0.0 reduce-scatter.7.cloned.1.call-update
  408.4 44.0 %reduce-scatter.7.cloned.1.call-done = f32[1024,4]{1,0:T(8,128)} async-done(((f32[4096,4]{1,0:T(8,128)}), f32[1024,4]{1,0:T(8,128)}) %reduce-scatter.7.cloned.1.call-update) | async-done | bytes 16400
  452.4 1.8 copy.16
  (2 shorter events, 0.0 us)
Async XLA Ops:
  7.4 268.5 %copy-start = (bf16[64,4096]{1,0:T(8,128)(2,1)S(1)}, bf16[64,4096]{1,0:T(8,128)(2,1)}, u32[]{:S(2)}) copy-start(bf16[64,4096]{1,0:T(8,128)(2,1)} %param.17) | copy-start | bytes 1572868
  7.4 85.9 %all-gather.4.cloned.1.call-start = ((), (), s32[]{:S(2)}) async-start(), calls=%async_computation.2 | async-start | bytes 5242880 | tf_op jit(solution)/shard_map/all_gather | solution.py:23
  8.1 265.9 %reduce-scatter.5.cloned.1.call-start = ((), (), s32[]{:S(2)}) async-start(), calls=%async_computation.3 | async-start | bytes 10485760 | tf_op jit(solution)/shard_map/reduce_scatter | solution.py:31
  93.3 14.7 %copy-start.3 = (bf16[512,4096]{1,0:T(8,128)(2,1)S(1)}, bf16[512,4096]{1,0:T(8,128)(2,1)}, u32[]{:S(2)}) copy-start(bf16[512,4096]{1,0:T(8,128)(2,1)} %all-gather.4.cloned.1.call-done) | copy-start | bytes 12582916
  93.3 27.5 %slice-start = ((s8[14680064]{0:T(1024)(128)(4,1)}), s8[4194304]{0:T(1024)(128)(4,1)S(1)}, s32[]{:S(2)}) async-start(s8[14680064]{0:T(1024)(128)(4,1)} %bitcast.33), calls=%async_computation.8 | async-start | bytes 8388608
  93.3 27.5 %slice-start.1 = ((s8[14680064]{0:T(1024)(128)(4,1)}), s8[4194304]{0:T(1024)(128)(4,1)S(1)}, s32[]{:S(2)}) async-start(s8[14680064]{0:T(1024)(128)(4,1)} %bitcast.33), calls=%async_computation.9 | async-start | bytes 8388608
  107.9 12.9 %slice-start.2 = ((s8[14680064]{0:T(1024)(128)(4,1)}), s8[4194304]{0:T(1024)(128)(4,1)S(1)}, s32[]{:S(2)}) async-start(s8[14680064]{0:T(1024)(128)(4,1)} %bitcast.33), calls=%async_computation.10 | async-start | bytes 8388608
  107.9 12.9 %slice-start.3 = ((s8[14680064]{0:T(1024)(128)(4,1)}), s8[2097152]{0:T(1024)(128)(4,1)S(1)}, s32[]{:S(2)}) async-start(s8[14680064]{0:T(1024)(128)(4,1)} %bitcast.33), calls=%async_computation.11 | async-start | bytes 4194304
  130.8 0.7 copy-start.2
  130.8 143.2 %copy-start.1 = (bf16[4,128,1024]{2,1,0:T(8,128)(2,1)S(1)}, bf16[4,128,1024]{2,1,0:T(8,128)(2,1)}, u32[]{:S(2)}) copy-start(bf16[4,128,1024]{2,1,0:T(8,128)(2,1)} %param.11) | copy-start | bytes 3145732
  130.8 182.5 %all-reduce.2.cloned.1.call-start = ((), (), s32[]{:S(2)}) async-start(), calls=%async_computation.4 | async-start | bytes 524288 | tf_op jit(solution)/shard_map/psum | solution.py:39
  277.1 61.0 %all-gather.6.cloned.1.call-start = ((), (), s32[]{:S(2)}) async-start(), calls=%async_computation.5 | async-start | bytes 10485760 | tf_op jit(solution)/shard_map/all_gather | solution.py:46
  277.7 120.1 %all-gather.8.cloned.1.call-start = ((), (), s32[]{:S(2)}) async-start(), calls=%async_computation.6 | async-start | bytes 10485760 | tf_op jit(solution)/shard_map/all_gather | solution.py:51
  278.3 174.1 %reduce-scatter.7.cloned.1.call-start = ((), (), s32[]{:S(2)}) async-start(), calls=%async_computation.7 | async-start | bytes 2621440
Sparse Core Ops, SparseCore 0:
  9.8 83.4 all-gather.3
  130.9 143.0 reduce-scatter.4
  277.2 36.0 all-reduce.1
  408.5 43.8 reduce-scatter.6
Sparse Core Ops, SparseCore 1:
  279.2 58.8 all-gather.5
  339.6 58.1 all-gather.7
where the time goes:
time: 462 us; the launch traced here: 461 us
  waiting for transfers between devices  390 us (84%)
  matrix products  50.4 us (11%)
  between operations  14.7 us (3%)
    reduce_scatter x1, waiting for transfers between devices, on_device(): lax.psum_scatter(partial_out, 'tensor', scatter_dimension=1, tiled=True)  141 us
    all_gather x1, waiting for transfers between devices, on_device(): piece = lax.all_gather(flat_tokens, 'tensor', axis=1, tiled=True)  85.1 us
    all_gather x1, waiting for transfers between devices, on_device(): lax.all_gather(test_sketches, 'clip', axis=0, tiled=True)  59.7 us
    unnamed x7, waiting for transfers between devices  45.8 us
    psum x1, waiting for transfers between devices, on_device(): lax.psum(jnp.concatenate([left_part, right_part], axis=1), 'tensor')  34.8 us
    all_gather x1, waiting for transfers between devices, on_device(): lax.all_gather(inv_hessian, 'clip', axis=0, tiled=True)  23.4 us
    dot_general x1, matrix products, on_device(): gate_act = jnp.dot(piece, gate_weight, preferred_element_type=jnp.float32)  14.7 us
    dot_general x1, matrix products, on_device(): up_act = jnp.dot(piece, up_weight, preferred_element_type=jnp.float32)  12.8 us
  transfers between devices with their start and end apart: 6, of which 6 were waited for; matrix products, arithmetic and copies ran while one was open for 1% of the time, Pallas kernels for 0%

commit v1 on v0

v1 whole, which is shorter than its diff:
```python
import functools

import jax
import jax.numpy as jnp
from jax import lax
from jax.experimental import pallas as pl
from jax.experimental.pallas import tpu as pltpu
from jax.sharding import PartitionSpec as P

MESH = pl.DeviceIdType.MESH


def entry_barrier(n, me):
    barrier = pltpu.get_barrier_semaphore()

    @pl.loop(0, n)
    def _(j):
        @pl.when(j != me)
        def _():
            pl.semaphore_signal(barrier, inc=1, device_id={"tensor": j}, device_id_type=MESH)

    pl.semaphore_wait(barrier, n - 1)


def layer_kernel(
    n,
    tile,
    clips_ref,
    targets_ref,
    weight_ref,
    gate_hbm,
    up_hbm,
    down_hbm,
    pin_ref,
    pout_ref,
    sketch_ref,
    gate_ref,
    up_ref,
    down_ref,
    tok,
    slots,
    hid,
    joined,
    parts,
    gathered,
    load_sem,
    ag_send,
    ag_recv,
    rs_send,
    rs_recv,
    own_send,
    own_recv,
    sk_send,
    sk_recv,
):
    me = lax.axis_index("tensor")
    count, rows, width = targets_ref.shape
    hidden_part = gate_ref.shape[1]
    last = n - 1
    tile_w = 256 if width % 256 == 0 else width

    own = pltpu.make_async_copy(clips_ref, tok.at[:, me], load_sem.at[0])
    own.start()
    loads = [
        pltpu.make_async_copy(gate_hbm, gate_ref, load_sem.at[1]),
        pltpu.make_async_copy(up_hbm, up_ref, load_sem.at[2]),
        pltpu.make_async_copy(down_hbm, down_ref, load_sem.at[3]),
    ]
    entry_barrier(n, me)
    own.wait()

    def token_copy(side, k, j):
        target = me + 1 if side == 0 else me - 1
        return pltpu.make_async_remote_copy(
            src_ref=tok.at[k, j],
            dst_ref=tok.at[k, j],
            send_sem=ag_send.at[side, k, j],
            recv_sem=ag_recv.at[k, j],
            device_id={"tensor": target},
            device_id_type=MESH,
        )

    def sum_copy(side, k, d):
        if side == 0:
            target, slot = me + 1, d
        else:
            target = me - 1
            slot = jnp.where(d == me - 1, n, d)
        return pltpu.make_async_remote_copy(
            src_ref=slots.at[k, d],
            dst_ref=slots.at[k, slot],
            send_sem=rs_send.at[k, d],
            recv_sem=rs_recv.at[k, slot],
            device_id={"tensor": target},
            device_id_type=MESH,
        )

    def wait_slot(k, slot):
        pltpu.make_async_copy(slots.at[k, slot], slots.at[k, slot], rs_recv.at[k, slot]).wait()

    def wait_token(k, j):
        pltpu.make_async_copy(tok.at[k, j], tok.at[k, j], ag_recv.at[k, j]).wait()

    def partial_tile(k, d, t):
        start = pl.multiple_of(d * width + t * tile_w, tile_w)
        return jnp.dot(
            hid[k], down_ref[:, pl.ds(start, tile_w)], preferred_element_type=jnp.float32
        )

    def add_and_send(side, k, d):
        first = me == (0 if side == 0 else last)

        @pl.when(first)
        def _():
            @pl.loop(0, width // tile_w)
            def _(t):
                cols = pl.ds(pl.multiple_of(t * tile_w, tile_w), tile_w)
                slots[k, d, :, cols] = partial_tile(k, d, t).astype(jnp.bfloat16)

        @pl.when(jnp.logical_not(first))
        def _():
            wait_slot(k, d)

            @pl.loop(0, width // tile_w)
            def _(t):
                cols = pl.ds(pl.multiple_of(t * tile_w, tile_w), tile_w)
                got = slots[k, d, :, cols].astype(jnp.float32)
                slots[k, d, :, cols] = (partial_tile(k, d, t) + got).astype(jnp.bfloat16)

        sum_copy(side, k, d).start()

    def forward_hidden(k):
        @pl.loop(0, hidden_part // tile)
        def _(t):
            cols = pl.ds(pl.multiple_of(t * tile, tile), tile)
            gate_act = jnp.zeros((rows, tile), jnp.float32)
            up_act = jnp.zeros((rows, tile), jnp.float32)
            for j in range(n):
                piece = tok[k, j]
                gate_act += jnp.dot(
                    piece,
                    gate_ref[j * width : (j + 1) * width, cols],
                    preferred_element_type=jnp.float32,
                )
                up_act += jnp.dot(
                    piece,
                    up_ref[j * width : (j + 1) * width, cols],
                    preferred_element_type=jnp.float32,
                )
            silu = gate_act / (1.0 + jnp.exp(-gate_act))
            hid[k, :, cols] = (silu * up_act).astype(jnp.bfloat16)

        joined[k] = jnp.dot(hid[k], pin_ref[...], preferred_element_type=jnp.float32)

    def finish(k):
        @pl.when(me > 0)
        def _():
            wait_slot(k, me)

        @pl.when(me < last)
        def _():
            wait_slot(k, n)

        from_left = jnp.where(me > 0, 1.0, 0.0)
        from_right = jnp.where(me < last, 1.0, 0.0)
        has_left = jnp.full((rows, tile_w), from_left, jnp.float32) > 0.5
        has_right = jnp.full((rows, tile_w), from_right, jnp.float32) > 0.5

        @pl.loop(0, width // tile_w)
        def _(t):
            cols = pl.ds(pl.multiple_of(t * tile_w, tile_w), tile_w)
            total = partial_tile(k, me, t)
            total += jnp.where(has_left, slots[k, me, :, cols].astype(jnp.float32), 0.0)
            total += jnp.where(has_right, slots[k, n, :, cols].astype(jnp.float32), 0.0)
            differ = jnp.clip(total - targets_ref[k, :, cols].astype(jnp.float32), -1.0, 1.0)
            grad = (differ * weight_ref[k]).astype(jnp.bfloat16)
            joined[k] += jnp.dot(
                grad, pout_ref[cols, :], preferred_element_type=jnp.float32
            )

        @pl.when(me != k)
        def _():
            part_copy(k).start()

    def part_copy(k):
        return pltpu.make_async_remote_copy(
            src_ref=joined.at[k],
            dst_ref=parts.at[me],
            send_sem=own_send.at[k],
            recv_sem=own_recv.at[me],
            device_id={"tensor": k},
            device_id_type=MESH,
        )

    def sketch_copy(j):
        return pltpu.make_async_remote_copy(
            src_ref=gathered.at[me],
            dst_ref=gathered.at[me],
            send_sem=sk_send.at[j],
            recv_sem=sk_recv.at[me],
            device_id={"tensor": j},
            device_id_type=MESH,
        )

    @pl.loop(0, count + 2 * last)
    def _(step):
        @pl.when(step < count)
        def _():
            @pl.when(me < last)
            def _():
                token_copy(0, step, me).start()

            @pl.when(me > 0)
            def _():
                token_copy(1, step, me).start()

        @pl.when(step == 0)
        def _():
            for load in loads:
                load.start()

        @pl.loop(1, n)
        def _(h):
            k = step - h

            @pl.when((k >= 0) & (k < count))
            def _():
                @pl.when(me - h >= 0)
                def _():
                    wait_token(k, me - h)

                    @pl.when(me < last)
                    def _():
                        token_copy(0, k, me - h).start()

                @pl.when(me + h <= last)
                def _():
                    wait_token(k, me + h)

                    @pl.when(me > 0)
                    def _():
                        token_copy(1, k, me + h).start()

        @pl.when(step == last)
        def _():
            for load in loads:
                load.wait()

        k_now = step - last

        @pl.when((k_now >= 0) & (k_now < count))
        def _():
            forward_hidden(k_now)

        k_right = step - last - me

        @pl.when((k_right >= 0) & (k_right < count))
        def _():
            @pl.loop(0, last - me)
            def _(i):
                add_and_send(0, k_right, last - i)

        k_left = step - last - (last - me)

        @pl.when((k_left >= 0) & (k_left < count))
        def _():
            @pl.loop(0, me)
            def _(d):
                add_and_send(1, k_left, d)

        k_end = step - 2 * last

        @pl.when((k_end >= 0) & (k_end < count))
        def _():
            finish(k_end)

    @pl.when(me < count)
    def _():
        total = joined[me]
        parts[me] = total

        @pl.loop(0, n)
        def _(j):
            @pl.when(j != me)
            def _():
                pltpu.make_async_copy(parts.at[j], parts.at[j], own_recv.at[j]).wait()

        total = parts[0]
        for j in range(1, n):
            total += parts[j]
        product = jnp.dot(
            total.T,
            total,
            precision=lax.Precision.HIGHEST,
            preferred_element_type=jnp.float32,
        )
        gathered[me] = product.astype(jnp.bfloat16)

        @pl.loop(0, n)
        def _(j):
            @pl.when(j != me)
            def _():
                sketch_copy(j).start()

    @pl.loop(0, count)
    def _(k):
        @pl.when(k != me)
        def _():
            pltpu.make_async_copy(gathered.at[k], gathered.at[k], sk_recv.at[k]).wait()

    sketch_ref[...] = gathered[...]

    @pl.when(me < count)
    def _():
        @pl.loop(0, n)
        def _(j):
            @pl.when(j != me)
            def _():
                sketch_copy(j).wait_send()

    @pl.loop(0, count)
    def _(k):
        @pl.when(k != me)
        def _():
            part_copy(k).wait_send()

        @pl.loop(0, n)
        def _(j):
            @pl.when((j <= me) & (me < last))
            def _():
                token_copy(0, k, j).wait_send()

            @pl.when((j >= me) & (me > 0))
            def _():
                token_copy(1, k, j).wait_send()

            @pl.when(j > me)
            def _():
                sum_copy(0, k, j).wait_send()

            @pl.when(j < me)
            def _():
                sum_copy(1, k, j).wait_send()


def scatter_kernel(n, x_ref, out_ref, pieces, send_sem, recv_sem, landed):
    me = lax.axis_index("tensor")
    width = out_ref.shape[1]
    for j in range(n):
        pieces[j] = x_ref[:, j * width : (j + 1) * width]
    entry_barrier(n, me)

    def copy(j):
        return pltpu.make_async_remote_copy(
            src_ref=pieces.at[j],
            dst_ref=landed.at[me],
            send_sem=send_sem.at[j],
            recv_sem=recv_sem.at[me],
            device_id={"tensor": j},
            device_id_type=MESH,
        )

    @pl.loop(0, n)
    def _(j):
        @pl.when(j != me)
        def _():
            copy(j).start()

    landed[me] = pieces[me]

    @pl.loop(0, n)
    def _(j):
        @pl.when(j != me)
        def _():
            pltpu.make_async_copy(landed.at[j], landed.at[j], recv_sem.at[j]).wait()

    total = landed[0]
    for j in range(1, n):
        total += landed[j]
    out_ref[...] = total

    @pl.loop(0, n)
    def _(j):
        @pl.when(j != me)
        def _():
            copy(j).wait_send()


def on_device(
    n,
    clips,
    targets,
    lengths,
    gate_weight,
    up_weight,
    down_weight,
    proj_in,
    proj_out,
    inv_hessian,
    test_sketches,
):
    count, rows, width = clips.shape
    hidden_part = gate_weight.shape[1]
    proj_size = proj_in.shape[0]
    full_hessian = lax.all_gather(inv_hessian, "clip", axis=0, tiled=True)
    full_tests = lax.all_gather(test_sketches, "clip", axis=0, tiled=True)

    position = jnp.arange(rows, dtype=jnp.int32)
    valid = (position[None, :] < lengths[:, None]).astype(jnp.float32)
    weight = (valid / lengths.astype(jnp.float32)[:, None])[:, :, None]
    start = lax.axis_index("tensor") * width
    proj_cols = lax.dynamic_slice_in_dim(proj_out, start, width, 1)
    pin = jnp.pad(proj_in.T, ((0, 0), (0, proj_size)))
    pout = jnp.pad(proj_cols.T, ((0, 0), (proj_size, 0)))
    both = 2 * proj_size

    tile = 256 if hidden_part % 256 == 0 else hidden_part
    vmem = pl.BlockSpec(memory_space=pltpu.VMEM)
    hbm = pl.BlockSpec(memory_space=pltpu.HBM)
    bf16, f32 = jnp.bfloat16, jnp.float32
    dma = pltpu.SemaphoreType.DMA
    sketches = pl.pallas_call(
        functools.partial(layer_kernel, n, tile),
        out_shape=jax.ShapeDtypeStruct((count, both, both), bf16),
        in_specs=[hbm, vmem, vmem, hbm, hbm, hbm, vmem, vmem],
        out_specs=vmem,
        scratch_shapes=[
            pltpu.VMEM(gate_weight.shape, bf16),
            pltpu.VMEM(up_weight.shape, bf16),
            pltpu.VMEM(down_weight.shape, bf16),
            pltpu.VMEM((count, n, rows, width), bf16),
            pltpu.VMEM((count, n + 1, rows, width), bf16),
            pltpu.VMEM((count, rows, hidden_part), bf16),
            pltpu.VMEM((count, rows, both), f32),
            pltpu.VMEM((n, rows, both), f32),
            pltpu.VMEM((count, both, both), bf16),
            dma((4,)),
            dma((2, count, n)),
            dma((count, n)),
            dma((count, n)),
            dma((count, n + 1)),
            dma((count,)),
            dma((n,)),
            dma((n,)),
            dma((count,)),
        ],
        compiler_params=pltpu.CompilerParams(
            collective_id=0, has_side_effects=True, vmem_limit_bytes=62 * 1024 * 1024
        ),
        cost_estimate=pl.CostEstimate(
            flops=6 * count * rows * hidden_part * width * n,
            bytes_accessed=400_000_000,
            transcendentals=count * rows * hidden_part,
        ),
        name="layer",
    )(clips, targets, weight, gate_weight, up_weight, down_weight, pin, pout)

    flat_sketch = sketches[:, :proj_size, proj_size:].reshape(count, proj_size * proj_size)
    precond = jnp.dot(
        flat_sketch, full_hessian, preferred_element_type=jnp.float32
    ).astype(jnp.bfloat16)
    partial_scores = lax.dot_general(
        precond,
        full_tests,
        (((1,), (1,)), ((), ())),
        preferred_element_type=jnp.float32,
    )
    out_width = partial_scores.shape[1] // n
    return pl.pallas_call(
        functools.partial(scatter_kernel, n),
        out_shape=jax.ShapeDtypeStruct((count, out_width), f32),
        in_specs=[vmem],
        out_specs=vmem,
        scratch_shapes=[
            pltpu.VMEM((n, count, out_width), f32),
            dma((n,)),
            dma((n,)),
            pltpu.VMEM((n, count, out_width), f32),
        ],
        compiler_params=pltpu.CompilerParams(collective_id=1, has_side_effects=True),
        name="scatter",
    )(partial_scores)


def solution(mesh):
    in_specs = (
        P(("parts", "clip"), None, "tensor"),
        P(("parts", "clip"), None, "tensor"),
        P(("parts", "clip")),
        P(None, "tensor"),
        P(None, "tensor"),
        P("tensor", None),
        P(None, "tensor"),
        P(),
        P("clip", "tensor"),
        P("clip", "tensor"),
    )
    out_specs = P(("parts", "clip"), "tensor")
    return jax.shard_map(
        functools.partial(on_device, mesh.shape["tensor"]),
        mesh=mesh,
        in_specs=in_specs,
        out_specs=out_specs,
        check_vma=False,
    )
```

time: 462 us -> 177 us (0.38)
  waiting for transfers between devices: 390 us -> 1.44 us
  Pallas kernels: 0 us -> 145 us
  matrix products: 50.4 us -> 9.75 us
    all_gather x3 -> x2, waiting for transfers between devices: 168 us -> 0.04 us  [the longest x1 0.02 us: on_device(): full_hessian = lax.all_gather(inv_hessian, 'clip', axis=0, tiled=True)]
    pallas_call x0 -> x2, Pallas kernels: none -> 145 us  [the longest x1 138 us: on_device(): pl.pallas_call(functools.partial(layer_kernel, n, tile), out_shape=jax.Sh...]
    reduce_scatter x1 -> x0, waiting for transfers between devices: 141 us -> none  [on_device(): lax.psum_scatter(partial_out, 'tensor', scatter_dimension=1, tiled=True)]
    unnamed x7 -> x2, waiting for transfers between devices: 45.8 us -> 1.41 us
    psum x1 -> x0, waiting for transfers between devices: 34.8 us -> none  [on_device(): lax.psum(jnp.concatenate([left_part, right_part], axis=1), 'tensor')]
    dot_general x6 -> x1, matrix products: 39.8 us -> 9.75 us  [on_device(): lax.dot_general(precond, full_tests, (((1,), (1,)), ((), ())), preferred_...]
    unnamed x1 -> x0, matrix products: 10.6 us -> none
  transfers between devices with their start and end apart: 6 -> 2, of which waited for: 6 -> 0; matrix products, arithmetic and copies ran while one was open for 1% -> 4% of each run, Pallas kernels for 0% -> 78%
where the time goes in v1:
time: 177 us
  Pallas kernels  145 us (82%)
  between operations  13.5 us (8%)
  matrix products  9.75 us (6%)
  local copies, waits for them, and re-layouts  5.47 us (3%)
  other arithmetic  2.11 us (1%)
    pallas_call x1, Pallas kernels, on_device(): pl.pallas_call(functools.partial(layer_kernel, n, tile), out_shape=jax.Sh...  138 us
    dot_general x1, matrix products, on_device(): lax.dot_general(precond, full_tests, (((1,), (1,)), ((), ())), preferred_...  9.75 us
    pallas_call x1, Pallas kernels, on_device(): pl.pallas_call(functools.partial(scatter_kernel, n), out_shape=jax.ShapeD...  7.06 us
  transfers between devices with their start and end apart: 2, of which 0 were waited for; matrix products, arithmetic and copies ran while one was open for 4% of the time, Pallas kernels for 78%

profile of v1, /device:TPU:0, one launch (start us, length us, event | category | flops | bytes accessed | tf_op | source)
XLA Modules:
  0.0 177.1 jit_solution(6563473738756462591)
XLA Ops:
  6.5 0.0 copy-start
  6.5 0.0 all-gather.3.cloned.1.call-start
  6.5 0.7 all-gather.3.cloned.1.call-update
  7.3 0.0 all-gather.5.cloned.1.call-start
  7.3 0.7 all-gather.5.cloned.1.call-update
  8.0 0.0 copy-done
  8.0 0.2 copy.16
  8.2 1.2 copy.14
  9.4 0.8 pad.9.pout_ref
  10.3 0.9 pad.8.pin_ref
  11.1 0.7 convert_element_type.21
  11.8 1.5 convert_divide_fusion.weight_ref
  13.2 137.8 %layer.1 = bf16[4,128,128]{2,1,0:T(8,128)(2,1)} custom-call(bf16[4,128,1024]{2,1,0:T(8,128)(2,1)} %clips_ref.1, bf16[4,128,1024]{2,1,0:T(8,128)(2,1)} %targets_ref.1, f32[4,128,1]{2,1,0:T(8,128)} %convert_divide_fusion.weight_ref, bf16[4096,1792]{1,0:T(8,128)(2,1)} %gate_hbm.1, bf16[4096,1792]{1,0:T(8,128)(2,1)} %up_hbm.1, bf16[1792,4096]{1,0:T(8,128)(2,1)} %down_hbm.1, ...), custom_call_target="tpu_custom_call" | custom-call | flops 22548578304 | bytes 400000000 | tf_op jit(solution)/shard_map/layer/pallas_call | solution.py:422
  151.1 0.9 slice.3
  152.0 0.0 copy-start.1
  152.0 0.1 reshape.62
  152.1 0.0 all-gather.3.cloned.1.call-done
  152.1 0.0 all-gather.5.cloned.1.call-done
  152.2 9.7 %fusion.x_ref = f32[4,4096]{1,0:T(4,128)} fusion(bf16[4096,1024]{1,0:T(8,128)(2,1)} %all-gather.5.cloned.1.call-done, bf16[4,4096]{1,0:T(4,128)(2,1)S(1)} %reshape.62, bf16[4096,1024]{1,0:T(8,128)(2,1)} %all-gather.3.cloned.1.call-done), kind=kOutput, calls=%fused_computation.1 | convolution fusion | flops 67112960 | bytes 16875520 | tf_op jit(solution)/shard_map/dot_general | solution.py:462
  161.9 7.1 %scatter.1 = f32[4,1024]{1,0:T(4,128)} custom-call(f32[4,4096]{1,0:T(4,128)} %fusion.x_ref), custom_call_target="tpu_custom_call" | custom-call | tf_op jit(solution)/shard_map/scatter/pallas_call | solution.py:469
  169.0 1.3 copy.19
  170.3 0.0 copy-done.1
  (1 shorter events, 0.0 us)
Async XLA Ops:
  6.5 1.5 copy-start
  6.5 145.6 %all-gather.3.cloned.1.call-start = ((), (), s32[]{:S(2)}) async-start(), calls=%async_computation | async-start | bytes 10485760 | tf_op jit(solution)/shard_map/all_gather | solution.py:405
  7.3 144.9 %all-gather.5.cloned.1.call-start = ((), (), s32[]{:S(2)}) async-start(), calls=%async_computation.1 | async-start | bytes 10485760 | tf_op jit(solution)/shard_map/all_gather | solution.py:406
  152.0 18.3 %copy-start.1 = (bf16[64,4096]{1,0:T(8,128)(2,1)S(1)}, bf16[64,4096]{1,0:T(8,128)(2,1)}, u32[]{:S(2)}) copy-start(bf16[64,4096]{1,0:T(8,128)(2,1)} %param.17) | copy-start | bytes 1572868
Sparse Core Ops, SparseCore 0:
  8.9 60.9 all-gather.2
  71.5 58.2 all-gather.4

commit v2 on v1

--- a/solution.py
+++ b/solution.py
@@ -343,50 +343,159 @@
                 sum_copy(1, k, j).wait_send()
 
 
-def scatter_kernel(n, x_ref, out_ref, pieces, send_sem, recv_sem, landed):
+def score_kernel(
+    nc,
+    n,
+    flat_ref,
+    hessian_ref,
+    tests_ref,
+    out_ref,
+    pieces,
+    landed_pieces,
+    stacked,
+    partial,
+    landed_partial,
+    blocks,
+    landed_blocks,
+    send_a,
+    recv_a,
+    send_b,
+    recv_b,
+    send_c,
+    recv_c,
+):
+    my_clip = lax.axis_index("clip")
     me = lax.axis_index("tensor")
-    width = out_ref.shape[1]
-    for j in range(n):
-        pieces[j] = x_ref[:, j * width : (j + 1) * width]
-    entry_barrier(n, me)
-
-    def copy(j):
+    count, out_width = out_ref.shape
+    depth = hessian_ref.shape[0]
+    ratio = n // nc
+
+    barrier = pltpu.get_barrier_semaphore()
+
+    @pl.loop(0, nc)
+    def _(c):
+        @pl.loop(0, n)
+        def _(z):
+            @pl.when((c != my_clip) | (z != me))
+            def _():
+                pl.semaphore_signal(
+                    barrier, inc=1, device_id={"clip": c, "tensor": z}, device_id_type=MESH
+                )
+
+    for c in range(nc):
+        pieces[c] = flat_ref[:, c * depth : (c + 1) * depth].astype(jnp.float32)
+    pl.semaphore_wait(barrier, nc * n - 1)
+
+    def piece_copy(c):
         return pltpu.make_async_remote_copy(
-            src_ref=pieces.at[j],
-            dst_ref=landed.at[me],
-            send_sem=send_sem.at[j],
-            recv_sem=recv_sem.at[me],
-            device_id={"tensor": j},
+            src_ref=pieces.at[c],
+            dst_ref=landed_pieces.at[my_clip],
+            send_sem=send_a.at[c],
+            recv_sem=recv_a.at[my_clip],
+            device_id={"clip": c, "tensor": me},
             device_id_type=MESH,
         )
 
+    def partial_copy(c):
+        return pltpu.make_async_remote_copy(
+            src_ref=partial,
+            dst_ref=landed_partial.at[my_clip],
+            send_sem=send_b.at[c],
+            recv_sem=recv_b.at[my_clip],
+            device_id={"clip": c, "tensor": me},
+            device_id_type=MESH,
+        )
+
+    def block_copy(c, q):
+        return pltpu.make_async_remote_copy(
+            src_ref=blocks.at[c, q],
+            dst_ref=landed_blocks.at[me],
+            send_sem=send_c.at[c, q],
+            recv_sem=recv_c.at[me],
+            device_id={"clip": c, "tensor": my_clip * ratio + q},
+            device_id_type=MESH,
+        )
+
+    def other_clips(act):
+        @pl.loop(0, nc)
+        def _(c):
+            @pl.when(c != my_clip)
+            def _():
+                act(c)
+
+    def wait_for(ref, sem):
+        pltpu.make_async_copy(ref, ref, sem).wait()
+
+    other_clips(lambda c: piece_copy(c).start())
+    landed_pieces[my_clip] = pieces[my_clip]
+    other_clips(lambda c: wait_for(landed_pieces.at[c], recv_a.at[c]))
+    for c in range(nc):
+        stacked[c * count : (c + 1) * count, :] = landed_pieces[c]
+    partial[...] = jnp.dot(
+        stacked[...].astype(jnp.bfloat16),
+        hessian_ref[...],
+        preferred_element_type=jnp.float32,
+    )
+    other_clips(lambda c: partial_copy(c).start())
+    landed_partial[my_clip] = partial[...]
+    other_clips(lambda c: wait_for(landed_partial.at[c], recv_b.at[c]))
+    precond = landed_partial[0]
+    for c in range(1, nc):
+        precond += landed_partial[c]
+    scores = lax.dot_general(
+        precond.astype(jnp.bfloat16),
+        tests_ref[...],
+        (((1,), (1,)), ((), ())),
+        preferred_element_type=jnp.float32,
+    )
+    for c in range(nc):
+        for q in range(ratio):
+            blocks[c, q] = scores[
+                c * count : (c + 1) * count, q * out_width : (q + 1) * out_width
+            ]
+
+    def elsewhere(c, q):
+        return (c != my_clip) | (my_clip * ratio + q != me)
+
+    @pl.loop(0, nc)
+    def _(c):
+        @pl.loop(0, ratio)
+        def _(q):
+            @pl.when(elsewhere(c, q))
+            def _():
+                block_copy(c, q).start()
+
+            @pl.when(jnp.logical_not(elsewhere(c, q)))
+            def _():
+                landed_blocks[me] = blocks[c, q]
+
+    holds_own = (me >= my_clip * ratio) & (me < (my_clip + 1) * ratio)
+
     @pl.loop(0, n)
-    def _(j):
-        @pl.when(j != me)
-        def _():
-            copy(j).start()
-
-    landed[me] = pieces[me]
-
-    @pl.loop(0, n)
-    def _(j):
-        @pl.when(j != me)
-        def _():
-            pltpu.make_async_copy(landed.at[j], landed.at[j], recv_sem.at[j]).wait()
-
-    total = landed[0]
-    for j in range(1, n):
-        total += landed[j]
+    def _(z):
+        @pl.when((z != me) | jnp.logical_not(holds_own))
+        def _():
+            wait_for(landed_blocks.at[z], recv_c.at[z])
+
+    total = landed_blocks[0]
+    for z in range(1, n):
+        total += landed_blocks[z]
     out_ref[...] = total
 
-    @pl.loop(0, n)
-    def _(j):
-        @pl.when(j != me)
-        def _():
-            copy(j).wait_send()
+    other_clips(lambda c: piece_copy(c).wait_send())
+    other_clips(lambda c: partial_copy(c).wait_send())
+
+    @pl.loop(0, nc)
+    def _(c):
+        @pl.loop(0, ratio)
+        def _(q):
+            @pl.when(elsewhere(c, q))
+            def _():
+                block_copy(c, q).wait_send()
 
 
 def on_device(
+    nc,
     n,
     clips,
     targets,
@@ -402,9 +511,6 @@
     count, rows, width = clips.shape
     hidden_part = gate_weight.shape[1]
     proj_size = proj_in.shape[0]
-    full_hessian = lax.all_gather(inv_hessian, "clip", axis=0, tiled=True)
-    full_tests = lax.all_gather(test_sketches, "clip", axis=0, tiled=True)
-
     position = jnp.arange(rows, dtype=jnp.int32)
     valid = (position[None, :] < lengths[:, None]).astype(jnp.float32)
     weight = (valid / lengths.astype(jnp.float32)[:, None])[:, :, None]
@@ -456,30 +562,35 @@
     )(clips, targets, weight, gate_weight, up_weight, down_weight, pin, pout)
 
     flat_sketch = sketches[:, :proj_size, proj_size:].reshape(count, proj_size * proj_size)
-    precond = jnp.dot(
-        flat_sketch, full_hessian, preferred_element_type=jnp.float32
-    ).astype(jnp.bfloat16)
-    partial_scores = lax.dot_general(
-        precond,
-        full_tests,
-        (((1,), (1,)), ((), ())),
-        preferred_element_type=jnp.float32,
-    )
-    out_width = partial_scores.shape[1] // n
+    depth, columns = inv_hessian.shape
+    tests = test_sketches.shape[0]
+    ratio = n // nc
+    out_width = tests // ratio
     return pl.pallas_call(
-        functools.partial(scatter_kernel, n),
+        functools.partial(score_kernel, nc, n),
         out_shape=jax.ShapeDtypeStruct((count, out_width), f32),
-        in_specs=[vmem],
+        in_specs=[vmem, vmem, vmem],
         out_specs=vmem,
         scratch_shapes=[
+            pltpu.VMEM((nc, count, depth), f32),
+            pltpu.VMEM((nc, count, depth), f32),
+            pltpu.VMEM((nc * count, depth), f32),
+            pltpu.VMEM((nc * count, columns), f32),
+            pltpu.VMEM((nc, nc * count, columns), f32),
+            pltpu.VMEM((nc, ratio, count, out_width), f32),
             pltpu.VMEM((n, count, out_width), f32),
+            dma((nc,)),
+            dma((nc,)),
+            dma((nc,)),
+            dma((nc,)),
+            dma((nc, ratio)),
             dma((n,)),
-            dma((n,)),
-            pltpu.VMEM((n, count, out_width), f32),
         ],
-        compiler_params=pltpu.CompilerParams(collective_id=1, has_side_effects=True),
-        name="scatter",
-    )(partial_scores)
+        compiler_params=pltpu.CompilerParams(
+            collective_id=1, has_side_effects=True, vmem_limit_bytes=32 * 1024 * 1024
+        ),
+        name="tail",
+    )(flat_sketch, inv_hessian, test_sketches)
 
 
 def solution(mesh):
@@ -497,7 +608,7 @@
     )
     out_specs = P(("parts", "clip"), "tensor")
     return jax.shard_map(
-        functools.partial(on_device, mesh.shape["tensor"]),
+        functools.partial(on_device, mesh.shape["clip"], mesh.shape["tensor"]),
         mesh=mesh,
         in_specs=in_specs,
         out_specs=out_specs,

time: 177 us -> 164 us (0.927)
  between operations: 13.5 us -> 0.05 us
  matrix products: 9.75 us -> 0 us
  Pallas kernels: 145 us -> 152 us
  local copies, waits for them, and re-layouts: 5.47 us -> 8.99 us
    dot_general x1 -> x0, matrix products: 9.75 us -> none  [on_device(): lax.dot_general(precond, full_tests, (((1,), (1,)), ((), ())), preferred_...]
    pallas_call x1, Pallas kernels: 7.06 us -> 14.6 us  [on_device(): pl.pallas_call(functools.partial(score_kernel, nc, n), out_shape=jax.Shap...]
    unnamed x7 -> x9, local copies, waits for them, and re-layouts: 2.71 us -> 6.2 us
  transfers between devices with their start and end apart: 2 -> 0, of which waited for: 0 -> 0; matrix products, arithmetic and copies ran while one was open for 4% -> 0% of each run, Pallas kernels for 78% -> 0%
where the time goes in v2:
time: 164 us; the launch traced here: 163 us
  Pallas kernels  152 us (93%)
  local copies, waits for them, and re-layouts  8.99 us (5%)
  other arithmetic  2.11 us (1%)
    pallas_call x1, Pallas kernels, on_device(): pl.pallas_call(functools.partial(layer_kernel, n, tile), out_shape=jax.Sh...  138 us
    pallas_call x1, Pallas kernels, on_device(): pl.pallas_call(functools.partial(score_kernel, nc, n), out_shape=jax.Shap...  14.6 us
    unnamed x9, local copies, waits for them, and re-layouts  6.2 us

profile of v2, /device:TPU:0, one launch (start us, length us, event | category | flops | bytes accessed | tf_op | source)
XLA Modules:
  0.0 163.4 jit_solution(6547403463596749068)
XLA Ops:
  0.0 0.0 copy-start
  0.0 1.0 copy-done
  1.1 0.2 copy.16
  1.2 0.9 pad.9.pout_ref
  2.1 1.2 copy.14
  3.3 0.9 pad.8.pin_ref
  4.2 0.7 convert_element_type.18
  4.8 1.5 convert_divide_fusion.weight_ref
  6.3 137.6 %layer.1 = bf16[4,128,128]{2,1,0:T(8,128)(2,1)} custom-call(bf16[4,128,1024]{2,1,0:T(8,128)(2,1)} %clips_ref.1, bf16[4,128,1024]{2,1,0:T(8,128)(2,1)} %targets_ref.1, f32[4,128,1]{2,1,0:T(8,128)} %convert_divide_fusion.weight_ref, bf16[4096,1792]{1,0:T(8,128)(2,1)} %gate_hbm.1, bf16[4096,1792]{1,0:T(8,128)(2,1)} %up_hbm.1, bf16[1792,4096]{1,0:T(8,128)(2,1)} %down_hbm.1, ...), custom_call_target="tpu_custom_call" | custom-call | flops 22548578304 | bytes 400000000 | tf_op jit(solution)/shard_map/layer/pallas_call | solution.py:528
  143.9 0.9 slice.3
  144.9 0.1 reshape.62.flat_ref
  145.0 0.0 copy-start.1
  145.0 1.6 copy-done.1
  146.6 0.0 copy-start.2
  146.6 1.6 copy-done.2
  148.2 14.6 %tail.1 = f32[4,1024]{1,0:T(4,128)S(1)} custom-call(bf16[4,4096]{1,0:T(4,128)(2,1)S(1)} %reshape.62.flat_ref, bf16[1024,1024]{1,0:T(8,128)(2,1)S(1)} %copy-done.1, bf16[1024,1024]{1,0:T(8,128)(2,1)S(1)} %copy-done.2), custom_call_target="tpu_custom_call" | custom-call | tf_op jit(solution)/shard_map/tail/pallas_call | solution.py:569
  162.8 0.6 copy.19
  (1 shorter events, 0.0 us)
Async XLA Ops:
  0.0 1.0 copy-start
  145.0 1.6 copy-start.1
  146.6 1.6 copy-start.2

commit v3 on v2

--- a/solution.py
+++ b/solution.py
@@ -27,13 +27,15 @@
     tile,
     clips_ref,
     targets_ref,
-    weight_ref,
+    lengths_ref,
     gate_hbm,
     up_hbm,
     down_hbm,
+    pin_hbm,
+    pout_hbm,
+    sketch_ref,
     pin_ref,
     pout_ref,
-    sketch_ref,
     gate_ref,
     up_ref,
     down_ref,
@@ -56,6 +58,7 @@
     me = lax.axis_index("tensor")
     count, rows, width = targets_ref.shape
     hidden_part = gate_ref.shape[1]
+    proj = pin_hbm.shape[0]
     last = n - 1
     tile_w = 256 if width % 256 == 0 else width
 
@@ -65,7 +68,15 @@
         pltpu.make_async_copy(gate_hbm, gate_ref, load_sem.at[1]),
         pltpu.make_async_copy(up_hbm, up_ref, load_sem.at[2]),
         pltpu.make_async_copy(down_hbm, down_ref, load_sem.at[3]),
+        pltpu.make_async_copy(pin_hbm, pin_ref.at[pl.ds(0, proj)], load_sem.at[4]),
+        pltpu.make_async_copy(
+            pout_hbm.at[:, pl.ds(pl.multiple_of(me * width, width), width)],
+            pout_ref.at[pl.ds(proj, proj)],
+            load_sem.at[5],
+        ),
     ]
+    pin_ref[proj:, :] = jnp.zeros((proj, hidden_part), jnp.bfloat16)
+    pout_ref[:proj, :] = jnp.zeros((proj, width), jnp.bfloat16)
     entry_barrier(n, me)
     own.wait()
 
@@ -150,7 +161,12 @@
             silu = gate_act / (1.0 + jnp.exp(-gate_act))
             hid[k, :, cols] = (silu * up_act).astype(jnp.bfloat16)
 
-        joined[k] = jnp.dot(hid[k], pin_ref[...], preferred_element_type=jnp.float32)
+        joined[k] = lax.dot_general(
+            hid[k],
+            pin_ref[...],
+            (((1,), (1,)), ((), ())),
+            preferred_element_type=jnp.float32,
+        )
 
     def finish(k):
         @pl.when(me > 0)
@@ -165,6 +181,9 @@
         from_right = jnp.where(me < last, 1.0, 0.0)
         has_left = jnp.full((rows, tile_w), from_left, jnp.float32) > 0.5
         has_right = jnp.full((rows, tile_w), from_right, jnp.float32) > 0.5
+        length = jnp.full((rows, tile_w), lengths_ref[k], jnp.int32)
+        position = lax.broadcasted_iota(jnp.int32, (rows, tile_w), 0)
+        weight = jnp.where(position < length, 1.0 / length.astype(jnp.float32), 0.0)
 
         @pl.loop(0, width // tile_w)
         def _(t):
@@ -173,9 +192,12 @@
             total += jnp.where(has_left, slots[k, me, :, cols].astype(jnp.float32), 0.0)
             total += jnp.where(has_right, slots[k, n, :, cols].astype(jnp.float32), 0.0)
             differ = jnp.clip(total - targets_ref[k, :, cols].astype(jnp.float32), -1.0, 1.0)
-            grad = (differ * weight_ref[k]).astype(jnp.bfloat16)
-            joined[k] += jnp.dot(
-                grad, pout_ref[cols, :], preferred_element_type=jnp.float32
+            grad = (differ * weight).astype(jnp.bfloat16)
+            joined[k] += lax.dot_general(
+                grad,
+                pout_ref[:, cols],
+                (((1,), (1,)), ((), ())),
+                preferred_element_type=jnp.float32,
             )
 
         @pl.when(me != k)
@@ -347,9 +369,12 @@
     nc,
     n,
     flat_ref,
+    hessian_hbm,
+    tests_hbm,
+    out_ref,
     hessian_ref,
     tests_ref,
-    out_ref,
+    load_sem,
     pieces,
     landed_pieces,
     stacked,
@@ -370,6 +395,10 @@
     depth = hessian_ref.shape[0]
     ratio = n // nc
 
+    load_hessian = pltpu.make_async_copy(hessian_hbm, hessian_ref, load_sem.at[0])
+    load_tests = pltpu.make_async_copy(tests_hbm, tests_ref, load_sem.at[1])
+    load_hessian.start()
+    load_tests.start()
     barrier = pltpu.get_barrier_semaphore()
 
     @pl.loop(0, nc)
@@ -431,6 +460,7 @@
     other_clips(lambda c: wait_for(landed_pieces.at[c], recv_a.at[c]))
     for c in range(nc):
         stacked[c * count : (c + 1) * count, :] = landed_pieces[c]
+    load_hessian.wait()
     partial[...] = jnp.dot(
         stacked[...].astype(jnp.bfloat16),
         hessian_ref[...],
@@ -439,6 +469,7 @@
     other_clips(lambda c: partial_copy(c).start())
     landed_partial[my_clip] = partial[...]
     other_clips(lambda c: wait_for(landed_partial.at[c], recv_b.at[c]))
+    load_tests.wait()
     precond = landed_partial[0]
     for c in range(1, nc):
         precond += landed_partial[c]
@@ -511,26 +542,22 @@
     count, rows, width = clips.shape
     hidden_part = gate_weight.shape[1]
     proj_size = proj_in.shape[0]
-    position = jnp.arange(rows, dtype=jnp.int32)
-    valid = (position[None, :] < lengths[:, None]).astype(jnp.float32)
-    weight = (valid / lengths.astype(jnp.float32)[:, None])[:, :, None]
-    start = lax.axis_index("tensor") * width
-    proj_cols = lax.dynamic_slice_in_dim(proj_out, start, width, 1)
-    pin = jnp.pad(proj_in.T, ((0, 0), (0, proj_size)))
-    pout = jnp.pad(proj_cols.T, ((0, 0), (proj_size, 0)))
     both = 2 * proj_size
 
     tile = 256 if hidden_part % 256 == 0 else hidden_part
     vmem = pl.BlockSpec(memory_space=pltpu.VMEM)
     hbm = pl.BlockSpec(memory_space=pltpu.HBM)
+    smem = pl.BlockSpec(memory_space=pltpu.SMEM)
     bf16, f32 = jnp.bfloat16, jnp.float32
     dma = pltpu.SemaphoreType.DMA
     sketches = pl.pallas_call(
         functools.partial(layer_kernel, n, tile),
         out_shape=jax.ShapeDtypeStruct((count, both, both), bf16),
-        in_specs=[hbm, vmem, vmem, hbm, hbm, hbm, vmem, vmem],
+        in_specs=[hbm, vmem, smem, hbm, hbm, hbm, hbm, hbm],
         out_specs=vmem,
         scratch_shapes=[
+            pltpu.VMEM((both, hidden_part), bf16),
+            pltpu.VMEM((both, width), bf16),
             pltpu.VMEM(gate_weight.shape, bf16),
             pltpu.VMEM(up_weight.shape, bf16),
             pltpu.VMEM(down_weight.shape, bf16),
@@ -540,7 +567,7 @@
             pltpu.VMEM((count, rows, both), f32),
             pltpu.VMEM((n, rows, both), f32),
             pltpu.VMEM((count, both, both), bf16),
-            dma((4,)),
+            dma((6,)),
             dma((2, count, n)),
             dma((count, n)),
             dma((count, n)),
@@ -559,7 +586,7 @@
             transcendentals=count * rows * hidden_part,
         ),
         name="layer",
-    )(clips, targets, weight, gate_weight, up_weight, down_weight, pin, pout)
+    )(clips, targets, lengths, gate_weight, up_weight, down_weight, proj_in, proj_out)
 
     flat_sketch = sketches[:, :proj_size, proj_size:].reshape(count, proj_size * proj_size)
     depth, columns = inv_hessian.shape
@@ -569,9 +596,12 @@
     return pl.pallas_call(
         functools.partial(score_kernel, nc, n),
         out_shape=jax.ShapeDtypeStruct((count, out_width), f32),
-        in_specs=[vmem, vmem, vmem],
+        in_specs=[vmem, hbm, hbm],
         out_specs=vmem,
         scratch_shapes=[
+            pltpu.VMEM((depth, columns), bf16),
+            pltpu.VMEM(test_sketches.shape, bf16),
+            dma((2,)),
             pltpu.VMEM((nc, count, depth), f32),
             pltpu.VMEM((nc, count, depth), f32),
             pltpu.VMEM((nc * count, depth), f32),

time: 164 us -> 158 us (0.963)
  local copies, waits for them, and re-layouts: 8.99 us -> 4.83 us
  other arithmetic: 2.11 us -> 0 us
    unnamed x9 -> x5, local copies, waits for them, and re-layouts: 6.2 us -> 3.78 us
    pad x2 -> x0, local copies, waits for them, and re-layouts: 1.74 us -> none  [the longest x1 0.87 us: on_device(): pin = jnp.pad(proj_in.T, ((0, 0), (0, proj_size)))]
where the time goes in v3:
time: 158 us; the launch traced here: 157 us
  Pallas kernels  153 us (97%)
  local copies, waits for them, and re-layouts  4.83 us (3%)
    pallas_call x1, Pallas kernels, on_device(): pl.pallas_call(functools.partial(layer_kernel, n, tile), out_shape=jax.Sh...  137 us
    pallas_call x1, Pallas kernels, on_device(): pl.pallas_call(functools.partial(score_kernel, nc, n), out_shape=jax.Shap...  15 us
    unnamed x5, local copies, waits for them, and re-layouts  3.78 us

profile of v3, /device:TPU:0, one launch (start us, length us, event | category | flops | bytes accessed | tf_op | source)
XLA Modules:
  0.0 157.4 jit_solution(15829925736491593021)
XLA Ops:
  0.0 137.5 %layer.1 = bf16[4,128,128]{2,1,0:T(8,128)(2,1)} custom-call(bf16[4,128,1024]{2,1,0:T(8,128)(2,1)} %clips_ref.1, bf16[4,128,1024]{2,1,0:T(8,128)(2,1)} %targets_ref.1, s32[4]{0:T(128)} %lengths_ref.1, bf16[4096,1792]{1,0:T(8,128)(2,1)} %gate_hbm.1, bf16[4096,1792]{1,0:T(8,128)(2,1)} %up_hbm.1, bf16[1792,4096]{1,0:T(8,128)(2,1)} %down_hbm.1, ...), custom_call_target="tpu_custom_call" | custom-call | flops 22548578304 | bytes 400000000 | tf_op jit(solution)/shard_map/layer/pallas_call | solution.py:553
  137.5 0.9 slice.3
  138.4 0.1 reshape.3.flat_ref
  138.5 0.0 copy-start
  138.5 1.6 %copy-done = bf16[1024,1024]{1,0:T(8,128)(2,1)S(1)} copy-done((bf16[1024,1024]{1,0:T(8,128)(2,1)S(1)}, bf16[1024,1024]{1,0:T(8,128)(2,1)}, u32[]{:S(2)}) %copy-start) | copy-done | bytes 2097176
  140.1 0.0 copy-start.1
  140.1 1.6 %copy-done.1 = bf16[1024,1024]{1,0:T(8,128)(2,1)S(1)} copy-done((bf16[1024,1024]{1,0:T(8,128)(2,1)S(1)}, bf16[1024,1024]{1,0:T(8,128)(2,1)}, u32[]{:S(2)}) %copy-start.1) | copy-done | bytes 2097176
  141.7 15.0 %tail.1 = f32[4,1024]{1,0:T(4,128)S(1)} custom-call(bf16[4,4096]{1,0:T(4,128)(2,1)S(1)} %reshape.3.flat_ref, bf16[1024,1024]{1,0:T(8,128)(2,1)S(1)} %copy-done, bf16[1024,1024]{1,0:T(8,128)(2,1)S(1)} %copy-done.1), custom_call_target="tpu_custom_call" | custom-call | tf_op jit(solution)/shard_map/tail/pallas_call | solution.py:596
  156.8 0.6 copy.12
Async XLA Ops:
  138.5 1.6 %copy-start = (bf16[1024,1024]{1,0:T(8,128)(2,1)S(1)}, bf16[1024,1024]{1,0:T(8,128)(2,1)}, u32[]{:S(2)}) copy-start(bf16[1024,1024]{1,0:T(8,128)(2,1)} %hessian_hbm.1) | copy-start | bytes 6291460
  140.1 1.6 %copy-start.1 = (bf16[1024,1024]{1,0:T(8,128)(2,1)S(1)}, bf16[1024,1024]{1,0:T(8,128)(2,1)}, u32[]{:S(2)}) copy-start(bf16[1024,1024]{1,0:T(8,128)(2,1)} %tests_hbm.1) | copy-start | bytes 6291460
